TPU v7x, 256 devices: a whole 4x4x8 slice. The times are simulated.
256 devices in a mesh: col: 64 (over y, z, core), row: 4 (over x).
Axes of the slice: x: 4, y: 4, z: 8, core: 2. Of those that a mesh axis runs over, the one named last changes fastest.
Arguments:
- r_slab: float32 [1024, 16384], P('row', 'col'), may hold values from -4 to 8, as said below
- arc_rows: float32 [4096, 16384], P('row', 'col'), may hold values from -6 to 6
- arc_blocks: int32 [32, 64], P('row', 'col'), may hold values 0 or 1
Outputs:
- r_updated: float32 [1024, 16384], P('row', 'col')
Inputs may be any that keep to these rules, and one draw needn't show every extreme that they name: r_slab is zero wherever an entry's global column index is below its row index, and its diagonal is positive.
All inputs are finite; a program needn't handle non-finite values. No bound on the sum of `arc_blocks` on one device may be relied on, other than what follows from the above.
Results may differ from a plain program's by a relative error of at most 0.000098.
Values sent between devices are 32-bit elements; how exact they have to be, the bound alone decides.
A program may use at most 64 MiB of HBM per device.

v0:
```python
import jax
import jax.numpy as jnp
from jax import lax
from jax.sharding import PartitionSpec as P

B = 256
P_SIZE = 4
ARC_ROWS = 128
HI = lax.Precision.HIGHEST


def inner_dot(left, right):
    return lax.dot_general(left, right, (((0,), (0,)), ((), ())), precision=HI)


def plain_dot(left, right):
    return jnp.dot(left, right, precision=HI)


def on_device(r_slab, arc_rows, arc_blocks):
    n_col = lax.axis_size("col")
    col_index = lax.axis_index("col")
    row_index = lax.axis_index("row")
    n_arcs, blocks_here = arc_blocks.shape
    lead = P_SIZE * B
    live = arc_blocks.astype(jnp.float32)
    masked = (arc_rows.reshape(n_arcs, ARC_ROWS, blocks_here, B) * live[:, None, :, None]).reshape(
        arc_rows.shape
    )
    stacked = jnp.concatenate([r_slab, masked], axis=0)
    height = stacked.shape[0]
    part = height // n_col
    pieces = stacked.reshape(n_col, part, B)
    pieces = lax.all_to_all(pieces, "col", split_axis=0, concat_axis=0, tiled=True)
    mine = pieces[:P_SIZE]
    panels = lax.all_gather(mine, "col")
    panels = panels.transpose(0, 2, 1, 3).reshape(height, lead)
    share = lead // n_col
    own = lax.dynamic_slice(panels, (0, col_index * share), (height, share))
    gram_part = lax.psum(inner_dot(own, panels), "row")
    gram = lax.all_gather(gram_part, "col", tiled=True)
    rhs = lax.psum(inner_dot(panels, stacked), "row")
    lower = jnp.linalg.cholesky(gram, symmetrize_input=False)
    factor = jax.scipy.linalg.solve_triangular(lower, rhs, lower=True)
    mine_out = lax.dynamic_slice(factor, (row_index * B, 0), (B, B))
    row_ids = row_index * B + lax.broadcasted_iota(jnp.int32, (B, B), 0)
    col_ids = col_index * B + lax.broadcasted_iota(jnp.int32, (B, B), 1)
    return jnp.where(col_ids >= row_ids, mine_out, jnp.zeros_like(mine_out))


def solution(mesh):
    return jax.shard_map(
        on_device,
        mesh=mesh,
        in_specs=(P("row", "col"), P("row", "col"), P("row", "col")),
        out_specs=P("row", "col"),
        check_vma=False,
    )
```

profile of v0, /device:TPU:1, one launch (start us, length us, event | category | flops | bytes accessed | tf_op | source)
XLA Modules:
  0.0 636.5 jit_solution(12063077370027670616)
XLA Ops:
  12.2 52.7 %all_to_all.5 = f32[64,20,256]{2,1,0:T(8,128)S(1)} all-to-all(f32[64,20,256]{2,1,0:T(8,128)S(1)} %reshape.90), channel_id=1, replica_groups=mesh['col'=64,'row'=4] {'col'}, dimensions={0} | all-to-all | bytes 2621440 | tf_op jit(solution)/shard_map/all_to_all | solution.py:34
  65.7 78.4 %all-gather.6.cloned.1.call-done = f32[256,20,256]{2,1,0:T(8,128)} async-done(((f32[4,20,256]{2,1,0:T(8,128)}), f32[256,20,256]{2,1,0:T(8,128)}) %all-gather.6.cloned.1.call-update) | async-done | bytes 5242896 | tf_op jit(solution)/shard_map/all_gather | solution.py:36
  144.1 5.2 copy.5
  150.5 9.5 %fusion.63 = f32[1024,256]{1,0:T(8,128)} fusion(f32[1280,1024]{1,0:T(8,128)S(1)} %bitcast.108, f32[1024,256]{1,0:T(8,128)S(1)} %broadcast_multiply_fusion, f32[256,256]{1,0:T(8,128)S(1)} %copy-done), kind=kOutput, calls=%fused_computation.162 | convolution fusion | flops 4026859520 | bytes 7602176 | tf_op jit(solution)/shard_map/dot_general | solution.py:13
  160.1 14.3 %fusion.5 = f32[16,1024]{1,0:T(8,128)} fusion(f32[1280,1024]{1,0:T(8,128)S(1)} %bitcast.109, s32[]{:T(128)S(6)} %select_n.14), kind=kOutput, calls=%fused_computation.31 | convolution fusion | flops 251658240 | bytes 5963780 | tf_op jit(solution)/shard_map/dot_general | solution.py:13
  174.4 46.4 %all-reduce.4.cloned.1.call-done = (f32[1024,256]{1,0:T(8,128)}, f32[16,1024]{1,0:T(8,128)}) async-done(((f32[1024,256]{1,0:T(8,128)}, f32[16,1024]{1,0:T(8,128)}), (f32[1024,256]{1,0:T(8,128)}, f32[16,1024]{1,0:T(8,128)})) %all-reduce.4.cloned.1.call-update) | async-done | bytes 1114128 | tf_op jit(solution)/shard_map/psum | solution.py:42
  220.8 84.7 %all-gather.4.cloned.1.call-done = f32[1024,1024]{1,0:T(8,128)} async-done(((f32[16,1024]{1,0:T(8,128)}), f32[1024,1024]{1,0:T(8,128)}) %all-gather.4.cloned.1.call-update) | async-done | bytes 4194320 | tf_op jit(solution)/shard_map/all_gather | solution.py:41
  306.4 11.7 %cholesky.223 = f32[128,128]{1,0:T(8,128)S(1)} custom-call(f32[128,128]{1,0:T(8,128)S(1)} %cholesky.580), custom_call_target="Cholesky" | custom-call | tf_op jit(solution)/shard_map/jit(cholesky)/cholesky | solution.py:43
  318.1 9.8 %custom-call.63 = f32[1,128,128]{1,2,0:T(8,128)S(1)} custom-call(f32[1,128,128]{2,1,0:T(8,128)S(1)} %get-tuple-element.71), custom_call_target="InvertDiagBlocksLowerTriangular" | custom-call | tf_op jit(solution)/shard_map/jit(cholesky)/cholesky | solution.py:43
  328.0 2.5 cholesky.255
  330.5 2.4 constant_dynamic-update-slice_fusion.31
  334.4 11.7 %cholesky.244 = f32[128,128]{1,0:T(8,128)S(1)} custom-call(f32[128,128]{1,0:T(8,128)S(1)} %cholesky.584), custom_call_target="Cholesky" | custom-call | tf_op jit(solution)/shard_map/jit(cholesky)/cholesky | solution.py:43
  346.8 10.2 %custom-call.64 = f32[1,128,128]{1,2,0:T(8,128)S(1)} custom-call(f32[1,128,128]{2,1,0:T(8,128)S(1)} %get-tuple-element.68), custom_call_target="InvertDiagBlocksLowerTriangular" | custom-call | tf_op jit(solution)/shard_map/jit(cholesky)/cholesky | solution.py:43
  360.3 11.7 %cholesky.468 = f32[128,128]{1,0:T(8,128)S(1)} custom-call(f32[128,128]{1,0:T(8,128)S(1)} %cholesky.589), custom_call_target="Cholesky" | custom-call | tf_op jit(solution)/shard_map/jit(cholesky)/cholesky | solution.py:43
  373.4 9.8 %custom-call.65 = f32[1,128,128]{1,2,0:T(8,128)S(1)} custom-call(f32[1,128,128]{2,1,0:T(8,128)S(1)} %get-tuple-element.65), custom_call_target="InvertDiagBlocksLowerTriangular" | custom-call | tf_op jit(solution)/shard_map/jit(cholesky)/cholesky | solution.py:43
  384.3 2.3 convolution_subtract_fusion.2
  386.7 11.9 %cholesky.487 = f32[128,128]{1,0:T(8,128)S(1)} custom-call(f32[128,128]{1,0:T(8,128)S(1)} %cholesky.594), custom_call_target="Cholesky" | custom-call | tf_op jit(solution)/shard_map/jit(cholesky)/cholesky | solution.py:43
  399.9 9.8 %custom-call.66 = f32[1,128,128]{1,2,0:T(8,128)S(1)} custom-call(f32[1,128,128]{2,1,0:T(8,128)S(1)} %get-tuple-element.62), custom_call_target="InvertDiagBlocksLowerTriangular" | custom-call | tf_op jit(solution)/shard_map/jit(cholesky)/cholesky | solution.py:43
  410.8 2.3 convolution_subtract_fusion.3
  413.2 11.7 %cholesky.506 = f32[128,128]{1,0:T(8,128)S(1)} custom-call(f32[128,128]{1,0:T(8,128)S(1)} %cholesky.599), custom_call_target="Cholesky" | custom-call | tf_op jit(solution)/shard_map/jit(cholesky)/cholesky | solution.py:43
  426.2 9.8 %custom-call.67 = f32[1,128,128]{1,2,0:T(8,128)S(1)} custom-call(f32[1,128,128]{2,1,0:T(8,128)S(1)} %get-tuple-element.59), custom_call_target="InvertDiagBlocksLowerTriangular" | custom-call | tf_op jit(solution)/shard_map/jit(cholesky)/cholesky | solution.py:43
  437.1 2.5 convolution_subtract_fusion.4
  439.6 11.7 %cholesky.526 = f32[128,128]{1,0:T(8,128)S(1)} custom-call(f32[128,128]{1,0:T(8,128)S(1)} %cholesky.604), custom_call_target="Cholesky" | custom-call | tf_op jit(solution)/shard_map/jit(cholesky)/cholesky | solution.py:43
  452.7 9.8 %custom-call.68 = f32[1,128,128]{1,2,0:T(8,128)S(1)} custom-call(f32[1,128,128]{2,1,0:T(8,128)S(1)} %get-tuple-element.56), custom_call_target="InvertDiagBlocksLowerTriangular" | custom-call | tf_op jit(solution)/shard_map/jit(cholesky)/cholesky | solution.py:43
  465.5 11.7 %cholesky.546 = f32[128,128]{1,0:T(8,128)S(1)} custom-call(f32[128,128]{1,0:T(8,128)S(1)} %cholesky.609), custom_call_target="Cholesky" | custom-call | tf_op jit(solution)/shard_map/jit(cholesky)/cholesky | solution.py:43
  478.5 10.2 %custom-call.69 = f32[1,128,128]{1,2,0:T(8,128)S(1)} custom-call(f32[1,128,128]{2,1,0:T(8,128)S(1)} %get-tuple-element.53), custom_call_target="InvertDiagBlocksLowerTriangular" | custom-call | tf_op jit(solution)/shard_map/jit(cholesky)/cholesky | solution.py:43
  491.3 11.7 %cholesky.564 = f32[128,128]{1,0:T(8,128)S(1)} custom-call(f32[128,128]{1,0:T(8,128)S(1)} %convolution_subtract_fusion.13), custom_call_target="Cholesky" | custom-call | tf_op jit(solution)/shard_map/jit(cholesky)/cholesky | solution.py:43
  510.1 4.9 select_select_fusion
  515.0 23.1 %while.1 = (s32[]{:T(128)}, f32[1024,1024]{1,0:T(8,128)}, s32[8,2]{0,1:T(2,128)S(1)}, f32[8,128,128]{2,1,0:T(8,128)S(1)}, s32[]{:T(128)}) while((s32[]{:T(128)}, f32[1024,1024]{1,0:T(8,128)}, s32[8,2]{0,1:T(2,128)S(1)}, f32[8,128,128]{2,1,0:T(8,128)S(1)}, s32[]{:T(128)}) %tuple.58), condition=%wide.while_cond, body=%wide.while_body.sunk | while | flops 2 | bytes 131181 | solution.py:44
  515.7 2.3 bitcast_dynamic-update-slice_fusion.2
  518.6 2.3 bitcast_dynamic-update-slice_fusion.2
  538.1 78.6 %custom-call.70 = f32[8,128,128]{1,2,0:T(8,128)S(1)} custom-call(f32[8,128,128]{2,1,0:T(8,128)S(1)} %get-tuple-element.12), custom_call_target="InvertDiagBlocksLowerTriangular" | custom-call | tf_op jit(solution)/shard_map/jit(_solve_triangular)/triangular_solve | solution.py:44
  (91 shorter events, 62.9 us)
Async XLA Ops:
  6.5 137.5 %all-gather.6.cloned.1.call-start = ((), (), s32[]{:S(2)}) async-start(), calls=%async_computation.2 | async-start | bytes 6389760 | tf_op jit(solution)/shard_map/all_gather | solution.py:36
  65.6 155.2 %all-reduce.4.cloned.1.call-start = ((), (), s32[]{:S(2)}) async-start(), calls=%async_computation.3 | async-start | bytes 2228224 | tf_op jit(solution)/shard_map/psum | solution.py:42
  149.2 1.3 copy-start
  174.4 131.2 %all-gather.4.cloned.1.call-start = ((), (), s32[]{:S(2)}) async-start(), calls=%async_computation.1 | async-start | bytes 4259840 | tf_op jit(solution)/shard_map/all_gather | solution.py:41
  510.1 106.6 %copy-start.1 = (f32[1024,256]{1,0:T(8,128)S(1)}, f32[1024,256]{1,0:T(8,128)}, u32[]{:S(2)}) copy-start(f32[1024,256]{1,0:T(8,128)} %get-tuple-element.21) | copy-start | bytes 3145732
Sparse Core Ops, SparseCore 0:
  65.7 78.2 all-gather.5
  174.5 46.2 all-reduce.3
  223.9 81.5 all-gather.3
where the time goes:
time: 647 us; the launch traced here: 636 us
  other arithmetic  261 us (40%)
  waiting for transfers between devices  210 us (32%)
  matrix products  59.2 us (9%)
  blocking collectives  52.7 us (8%)
  local copies, waits for them, and re-layouts  34.8 us (5%)
  between operations  18.8 us (3%)
    another operation x30, other arithmetic, on_device(): lower = jnp.linalg.cholesky(gram, symmetrize_input=False)  173 us
    all_gather x1, waiting for transfers between devices, on_device(): gram = lax.all_gather(gram_part, 'col', tiled=True)  84.7 us
    another operation x3, other arithmetic, on_device(): factor = jax.scipy.linalg.solve_triangular(lower, rhs, lower=True)  83.5 us
    all_gather x1, waiting for transfers between devices, on_device(): panels = lax.all_gather(mine, 'col')  78.4 us
    all_to_all x1, blocking collectives, on_device(): lax.all_to_all(pieces, 'col', split_axis=0, concat_axis=0, tiled=True)  52.7 us
    psum x1, waiting for transfers between devices, on_device(): rhs = lax.psum(inner_dot(panels, stacked), 'row')  46.4 us
    dot_general x2, matrix products, inner_dot(): return lax.dot_general(left, right, (((0,), (0,)), ((), ())), precision=HI)  23.8 us
    another operation x14, matrix products, on_device(): lower = jnp.linalg.cholesky(gram, symmetrize_input=False)  23.3 us
  transfers between devices with their start and end apart: 3, of which 3 were waited for; matrix products, arithmetic and copies ran while one was open for 0% of the time, Pallas kernels for 0%

commit v1 on v0

--- a/solution.py
+++ b/solution.py
@@ -39,7 +39,7 @@
     own = lax.dynamic_slice(panels, (0, col_index * share), (height, share))
     gram_part = lax.psum(inner_dot(own, panels), "row")
     gram = lax.all_gather(gram_part, "col", tiled=True)
-    rhs = lax.psum(inner_dot(panels, stacked), "row")
+    rhs = jnp.sum(lax.all_gather(inner_dot(panels, stacked), "row"), 0)
     lower = jnp.linalg.cholesky(gram, symmetrize_input=False)
     factor = jax.scipy.linalg.solve_triangular(lower, rhs, lower=True)
     mine_out = lax.dynamic_slice(factor, (row_index * B, 0), (B, B))

time: 647 us -> 673 us (1.040)
  waiting for transfers between devices: 210 us -> 241 us
  matrix products: 59.2 us -> 50.8 us
    all_gather x0 -> x1, waiting for transfers between devices: none -> 55.2 us  [on_device(): rhs = jnp.sum(lax.all_gather(inner_dot(panels, stacked), 'row'), 0)]
    psum x1, waiting for transfers between devices: 46.4 us -> 27.5 us  [on_device(): gram_part = lax.psum(inner_dot(own, panels), 'row')]
    dot_general x2, matrix products: 23.8 us -> 15.4 us  [inner_dot(): return lax.dot_general(left, right, (((0,), (0,)), ((), ())), precision=HI)]
  transfers between devices with their start and end apart: 3 -> 4, of which waited for: 3 -> 4; matrix products, arithmetic and copies ran while one was open for 0% -> 2% of each run, Pallas kernels for 0% -> 0%
where the time goes in v1:
time: 673 us; the launch traced here: 665 us
  other arithmetic  263 us (39%)
  waiting for transfers between devices  241 us (36%)
  blocking collectives  52.7 us (8%)
  matrix products  50.8 us (8%)
  local copies, waits for them, and re-layouts  37.1 us (6%)
  between operations  18.7 us (3%)
    another operation x30, other arithmetic, on_device(): lower = jnp.linalg.cholesky(gram, symmetrize_input=False)  172 us
    another operation x3, other arithmetic, on_device(): factor = jax.scipy.linalg.solve_triangular(lower, rhs, lower=True)  83.4 us
    all_gather x1, waiting for transfers between devices, on_device(): gram = lax.all_gather(gram_part, 'col', tiled=True)  80.4 us
    all_gather x1, waiting for transfers between devices, on_device(): panels = lax.all_gather(mine, 'col')  78.4 us
    all_gather x1, waiting for transfers between devices, on_device(): rhs = jnp.sum(lax.all_gather(inner_dot(panels, stacked), 'row'), 0)  55.2 us
    all_to_all x1, blocking collectives, on_device(): lax.all_to_all(pieces, 'col', split_axis=0, concat_axis=0, tiled=True)  52.7 us
    psum x1, waiting for transfers between devices, on_device(): gram_part = lax.psum(inner_dot(own, panels), 'row')  27.5 us
    another operation x14, matrix products, on_device(): lower = jnp.linalg.cholesky(gram, symmetrize_input=False)  23.3 us
  transfers between devices with their start and end apart: 4, of which 4 were waited for; matrix products, arithmetic and copies ran while one was open for 2% of the time, Pallas kernels for 0%

profile of v1, /device:TPU:1, one launch (start us, length us, event | category | flops | bytes accessed | tf_op | source)
XLA Modules:
  0.0 665.1 jit_solution(9641180798195656786)
XLA Ops:
  12.2 52.7 %all_to_all.5 = f32[64,20,256]{2,1,0:T(8,128)S(1)} all-to-all(f32[64,20,256]{2,1,0:T(8,128)S(1)} %reshape.90), channel_id=1, replica_groups=mesh['col'=64,'row'=4] {'col'}, dimensions={0} | all-to-all | bytes 2621440 | tf_op jit(solution)/shard_map/all_to_all | solution.py:34
  65.7 78.4 %all-gather.8.cloned.1.call-done = f32[256,20,256]{2,1,0:T(8,128)} async-done(((f32[4,20,256]{2,1,0:T(8,128)}), f32[256,20,256]{2,1,0:T(8,128)}) %all-gather.8.cloned.1.call-update) | async-done | bytes 5242896 | tf_op jit(solution)/shard_map/all_gather | solution.py:36
  144.1 5.2 copy.5
  152.8 3.6 fusion.5
  157.0 11.8 %fusion.63 = f32[1024,256]{1,0:T(8,128)} fusion(f32[1280,1024]{1,0:T(8,128)} %bitcast.110, f32[1024,256]{1,0:T(8,128)S(1)} %broadcast_multiply_fusion, f32[256,256]{1,0:T(8,128)S(1)} %copy-done.1), kind=kOutput, calls=%fused_computation.162 | convolution fusion | flops 4026859520 | bytes 7602176 | tf_op jit(solution)/shard_map/dot_general | solution.py:13
  169.1 27.5 %all-reduce.3.cloned.1.call-done = f32[16,1024]{1,0:T(8,128)} async-done(((f32[16,1024]{1,0:T(8,128)}), f32[16,1024]{1,0:T(8,128)}) %all-reduce.3.cloned.1.call-update) | async-done | bytes 65552 | tf_op jit(solution)/shard_map/psum | solution.py:40
  196.7 55.2 %all-gather.10.cloned.1.call-done = f32[4096,256]{1,0:T(8,128)} async-done(((f32[1024,256]{1,0:T(8,128)}), f32[4096,256]{1,0:T(8,128)}) %all-gather.10.cloned.1.call-update) | async-done | bytes 4194320 | tf_op jit(solution)/shard_map/all_gather | solution.py:42
  251.9 2.6 reduce_sum.9
  254.5 80.4 %all-gather.6.cloned.1.call-done = f32[1024,1024]{1,0:T(8,128)} async-done(((f32[16,1024]{1,0:T(8,128)}), f32[1024,1024]{1,0:T(8,128)}) %all-gather.6.cloned.1.call-update) | async-done | bytes 4194320 | tf_op jit(solution)/shard_map/all_gather | solution.py:41
  335.7 11.7 %cholesky.223 = f32[128,128]{1,0:T(8,128)S(1)} custom-call(f32[128,128]{1,0:T(8,128)S(1)} %cholesky.580), custom_call_target="Cholesky" | custom-call | tf_op jit(solution)/shard_map/jit(cholesky)/cholesky | solution.py:43
  347.4 2.5 cholesky.255
  349.9 9.8 %custom-call.63 = f32[1,128,128]{1,2,0:T(8,128)S(1)} custom-call(f32[1,128,128]{2,1,0:T(8,128)S(1)} %get-tuple-element.69), custom_call_target="InvertDiagBlocksLowerTriangular" | custom-call | tf_op jit(solution)/shard_map/jit(cholesky)/cholesky | solution.py:43
  359.7 2.4 constant_dynamic-update-slice_fusion.31
  363.7 11.7 %cholesky.244 = f32[128,128]{1,0:T(8,128)S(1)} custom-call(f32[128,128]{1,0:T(8,128)S(1)} %cholesky.584), custom_call_target="Cholesky" | custom-call | tf_op jit(solution)/shard_map/jit(cholesky)/cholesky | solution.py:43
  376.0 10.0 %custom-call.64 = f32[1,128,128]{1,2,0:T(8,128)S(1)} custom-call(f32[1,128,128]{2,1,0:T(8,128)S(1)} %get-tuple-element.66), custom_call_target="InvertDiagBlocksLowerTriangular" | custom-call | tf_op jit(solution)/shard_map/jit(cholesky)/cholesky | solution.py:43
  389.4 11.7 %cholesky.468 = f32[128,128]{1,0:T(8,128)S(1)} custom-call(f32[128,128]{1,0:T(8,128)S(1)} %cholesky.589), custom_call_target="Cholesky" | custom-call | tf_op jit(solution)/shard_map/jit(cholesky)/cholesky | solution.py:43
  401.7 9.8 %custom-call.65 = f32[1,128,128]{1,2,0:T(8,128)S(1)} custom-call(f32[1,128,128]{2,1,0:T(8,128)S(1)} %get-tuple-element.63), custom_call_target="InvertDiagBlocksLowerTriangular" | custom-call | tf_op jit(solution)/shard_map/jit(cholesky)/cholesky | solution.py:43
  412.7 2.3 convolution_subtract_fusion.2
  415.0 12.1 %cholesky.487 = f32[128,128]{1,0:T(8,128)S(1)} custom-call(f32[128,128]{1,0:T(8,128)S(1)} %cholesky.594), custom_call_target="Cholesky" | custom-call | tf_op jit(solution)/shard_map/jit(cholesky)/cholesky | solution.py:43
  427.8 9.8 %custom-call.66 = f32[1,128,128]{1,2,0:T(8,128)S(1)} custom-call(f32[1,128,128]{2,1,0:T(8,128)S(1)} %get-tuple-element.60), custom_call_target="InvertDiagBlocksLowerTriangular" | custom-call | tf_op jit(solution)/shard_map/jit(cholesky)/cholesky | solution.py:43
  438.7 2.3 convolution_subtract_fusion.3
  441.1 11.7 %cholesky.506 = f32[128,128]{1,0:T(8,128)S(1)} custom-call(f32[128,128]{1,0:T(8,128)S(1)} %cholesky.599), custom_call_target="Cholesky" | custom-call | tf_op jit(solution)/shard_map/jit(cholesky)/cholesky | solution.py:43
  453.4 9.8 %custom-call.67 = f32[1,128,128]{1,2,0:T(8,128)S(1)} custom-call(f32[1,128,128]{2,1,0:T(8,128)S(1)} %get-tuple-element.57), custom_call_target="InvertDiagBlocksLowerTriangular" | custom-call | tf_op jit(solution)/shard_map/jit(cholesky)/cholesky | solution.py:43
  464.3 2.5 convolution_subtract_fusion.4
  466.8 11.7 %cholesky.526 = f32[128,128]{1,0:T(8,128)S(1)} custom-call(f32[128,128]{1,0:T(8,128)S(1)} %cholesky.604), custom_call_target="Cholesky" | custom-call | tf_op jit(solution)/shard_map/jit(cholesky)/cholesky | solution.py:43
  479.1 9.8 %custom-call.68 = f32[1,128,128]{1,2,0:T(8,128)S(1)} custom-call(f32[1,128,128]{2,1,0:T(8,128)S(1)} %get-tuple-element.54), custom_call_target="InvertDiagBlocksLowerTriangular" | custom-call | tf_op jit(solution)/shard_map/jit(cholesky)/cholesky | solution.py:43
  491.9 11.7 %cholesky.546 = f32[128,128]{1,0:T(8,128)S(1)} custom-call(f32[128,128]{1,0:T(8,128)S(1)} %cholesky.609), custom_call_target="Cholesky" | custom-call | tf_op jit(solution)/shard_map/jit(cholesky)/cholesky | solution.py:43
  504.3 10.0 %custom-call.69 = f32[1,128,128]{1,2,0:T(8,128)S(1)} custom-call(f32[1,128,128]{2,1,0:T(8,128)S(1)} %get-tuple-element.51), custom_call_target="InvertDiagBlocksLowerTriangular" | custom-call | tf_op jit(solution)/shard_map/jit(cholesky)/cholesky | solution.py:43
  516.9 11.7 %cholesky.564 = f32[128,128]{1,0:T(8,128)S(1)} custom-call(f32[128,128]{1,0:T(8,128)S(1)} %convolution_subtract_fusion.13), custom_call_target="Cholesky" | custom-call | tf_op jit(solution)/shard_map/jit(cholesky)/cholesky | solution.py:43
  538.6 4.8 select_select_fusion
  543.4 23.2 %while.1 = (s32[]{:T(128)}, f32[1024,1024]{1,0:T(8,128)}, s32[8,2]{0,1:T(2,128)S(1)}, f32[8,128,128]{2,1,0:T(8,128)S(1)}, s32[]{:T(128)}) while((s32[]{:T(128)}, f32[1024,1024]{1,0:T(8,128)}, s32[8,2]{0,1:T(2,128)S(1)}, f32[8,128,128]{2,1,0:T(8,128)S(1)}, s32[]{:T(128)}) %tuple.57), condition=%wide.while_cond, body=%wide.while_body.sunk | while | flops 2 | bytes 131189 | solution.py:44
  566.6 78.6 %custom-call.70 = f32[8,128,128]{1,2,0:T(8,128)S(1)} custom-call(f32[8,128,128]{2,1,0:T(8,128)S(1)} %get-tuple-element.12), custom_call_target="InvertDiagBlocksLowerTriangular" | custom-call | tf_op jit(solution)/shard_map/jit(_solve_triangular)/triangular_solve | solution.py:44
  (96 shorter events, 70.2 us)
Async XLA Ops:
  6.5 137.5 %all-gather.8.cloned.1.call-start = ((), (), s32[]{:S(2)}) async-start(), calls=%async_computation.3 | async-start | bytes 6389760 | tf_op jit(solution)/shard_map/all_gather | solution.py:36
  65.6 131.0 %all-reduce.3.cloned.1.call-start = ((), (), s32[]{:S(2)}) async-start(), calls=%async_computation.1 | async-start | bytes 131072 | tf_op jit(solution)/shard_map/psum | solution.py:40
  150.5 2.3 copy-start
  150.5 6.5 copy-start.1
  156.4 95.4 %all-gather.10.cloned.1.call-start = ((), (), s32[]{:S(2)}) async-start(), calls=%async_computation.4 | async-start | bytes 5242880 | tf_op jit(solution)/shard_map/all_gather | solution.py:42
  168.9 165.9 %all-gather.6.cloned.1.call-start = ((), (), s32[]{:S(2)}) async-start(), calls=%async_computation.2 | async-start | bytes 4259840 | tf_op jit(solution)/shard_map/all_gather | solution.py:41
Sparse Core Ops, SparseCore 0:
  65.7 78.2 all-gather.7
  156.5 40.0 all-reduce.2
  198.6 53.2 all-gather.9
  254.9 79.8 all-gather.5
